TPU v7x, 32 devices: a whole 2x2x4 slice. The times are simulated.
32 devices in a mesh: prow: 4 (over z), pcol: 8 (over y, x, core).
Axes of the slice: x: 2, y: 2, z: 4, core: 2. Of those that a mesh axis runs over, the one named last changes fastest.
Arguments:
- anc_inverse: float32 [2048, 2048], P('pcol', 'prow')
- pattern_one: int32 [8, 4], replicated, may hold values from 0 to 7, as said below
- parents: int32 [8], replicated, may hold values from 0 to 7, as said below
- low_one: float32 [8, 1024, 256], P('pcol', 'prow'), may hold values from -2 to 2
- pivot_one: float32 [8, 256, 256], P('pcol'), may hold values from -4 to 4
- low_two: float32 [8, 1024, 256], P('pcol', 'prow'), may hold values from -2 to 2
- second_scaled_factor: float32 [8, 256, 256], P('pcol'), may hold values from -2 to 2
- second_pivot_inverse: float32 [8, 256, 256], P('pcol'), may hold values from -4 to 4
Outputs:
- column_one: float32 [8, 2048, 256], P('prow', 'pcol')
- diag_one: float32 [8, 256, 256], P('pcol')
- column_two: float32 [8, 2048, 256], P('prow', 'pcol')
- second_parent_inverse: float32 [8, 256, 256], P('pcol')
- second_diagonal_inverse: float32 [8, 256, 256], P('pcol')
Inputs may be any that keep to these rules, and one draw needn't show every extreme that they name: `pattern_one`: entry r of each row names an ancestor of process row r: it lies in r * 2 to r * 2 + 1; for each r, every ancestor of that range is entry r of exactly 4 rows. `parents`: every first-level supernode is the parent of exactly one second-level supernode.
All inputs are finite; a program needn't handle non-finite values.
Results may differ from a plain program's by a relative error of at most 0.000073.
Values sent between devices are 32-bit elements; how exact they have to be, the bound alone decides.
A program may use at most 128 MiB of HBM per device.

v0:
```python
import jax
import jax.numpy as jnp
from jax import lax
from jax.sharding import PartitionSpec as P


def batched(left, right):
    return jnp.einsum("kab,kbd->kad", left, right, precision=lax.Precision.HIGHEST)


def batched_left_t(left, right):
    return jnp.einsum("kba,kbd->kad", left, right, precision=lax.Precision.HIGHEST)


def pick_rows(hit_mask, count):
    total = hit_mask.shape[0]
    keys = jnp.where(hit_mask, 0, total).astype(jnp.int32) + jnp.arange(total, dtype=jnp.int32)
    chosen_rows = jnp.argsort(keys)[:count]
    valid = jnp.take(hit_mask, chosen_rows, axis=0).astype(jnp.float32)[:, None, None]
    return (chosen_rows, valid)


def body(
    anc_inverse,
    pattern_one,
    parents,
    low_one,
    pivot_one,
    low_two,
    second_scaled_factor,
    second_pivot_inverse,
):
    my_row = lax.axis_index("prow")
    my_col = lax.axis_index("pcol")
    row_count = lax.axis_size("prow")
    col_count = lax.axis_size("pcol")
    per_row_anc = col_count // row_count
    supernode_block_width = pivot_one.shape[1]
    per_col_one = pivot_one.shape[0]
    per_col_two = second_scaled_factor.shape[0]
    owned = anc_inverse.shape[1] // supernode_block_width
    zblocks = anc_inverse.reshape(supernode_block_width, owned, supernode_block_width).transpose(
        1, 0, 2
    )
    lowall = lax.all_gather(low_one, "pcol", axis=0, tiled=True)
    total_one = lowall.shape[0]
    owned_slot_list = lax.dynamic_index_in_dim(pattern_one, my_row, 1, keepdims=False)
    chosen = jnp.take(zblocks, owned_slot_list - my_row * owned, axis=0)
    first_terms = batched(chosen, lowall)
    lowsec, topall = (
        lax.all_gather(low_two, "pcol", axis=0, tiled=True),
        lax.all_gather(second_scaled_factor, "pcol", axis=0, tiled=True),
    )
    total_two = lowsec.shape[0]
    pattern_two = jnp.take(pattern_one, parents, axis=0)
    my_slots_two = lax.dynamic_index_in_dim(pattern_two, my_row, 1, keepdims=False)
    chosen_two = jnp.take(zblocks, my_slots_two - my_row * owned, axis=0)
    first_full = -lax.psum(first_terms, "prow")
    share = total_two // row_count
    start = my_row * share
    parents_share = lax.dynamic_slice_in_dim(parents, start, share, 0)
    tops_share = lax.dynamic_slice_in_dim(topall, start, share, 0)
    carried = batched(jnp.take(first_full, parents_share, axis=0), tops_share)
    base_terms = batched(chosen_two, lowsec)
    updated = lax.dynamic_slice_in_dim(base_terms, start, share, 0) + carried
    second_terms = lax.dynamic_update_slice_in_dim(base_terms, updated, start, 0)
    second_full = -lax.psum(second_terms, "prow")
    rows_one, valid_one = pick_rows(owned_slot_list == my_col, total_one // per_row_anc)
    pivot_small = valid_one * batched_left_t(
        jnp.take(lowall, rows_one, axis=0), jnp.take(first_full, rows_one, axis=0)
    )
    pivot_terms = jnp.zeros_like(first_full).at[rows_one].add(pivot_small)
    pivot_part = lax.psum_scatter(pivot_terms, "pcol", scatter_dimension=0, tiled=True)
    pivot_sum = lax.psum(pivot_part, "prow")
    diag_one = pivot_one - pivot_sum
    count_one = first_full.shape[0] // row_count
    column_one = lax.dynamic_slice_in_dim(first_full, my_row * count_one, count_one, 0)
    second_level_count = second_full.shape[0] // row_count
    column_two = lax.dynamic_slice_in_dim(
        second_full, my_row * second_level_count, second_level_count, 0
    )
    rows_two, valid_two = pick_rows(my_slots_two == my_col, total_two // per_row_anc)
    lows_picked = jnp.take(lowsec, rows_two, axis=0)
    parent_picked = jnp.take(first_full, jnp.take(parents, rows_two, axis=0), axis=0)
    cross_small = valid_two * batched_left_t(parent_picked, lows_picked)
    diag_small = valid_two * batched_left_t(lows_picked, jnp.take(second_full, rows_two, axis=0))
    local_parent = parents - my_col * per_col_one
    own_parent = (local_parent >= 0) & (local_parent < per_col_one)
    rows_own, valid_own = pick_rows(own_parent, per_col_two)
    valid_own = valid_own * (my_row == 0).astype(jnp.float32)
    local_picked = jnp.clip(jnp.take(local_parent, rows_own, axis=0), 0, per_col_one - 1)
    picked = jnp.take(diag_one, local_picked, axis=0)
    own_small = valid_own * batched(picked, jnp.take(topall, rows_own, axis=0))
    cross_terms = (
        jnp.zeros_like(second_full).at[rows_two].add(cross_small).at[rows_own].add(own_small)
    )
    diag_terms = jnp.zeros_like(second_full).at[rows_two].add(diag_small)
    part_cross, part_diag = (
        lax.psum_scatter(cross_terms, "pcol", scatter_dimension=0, tiled=True),
        lax.psum_scatter(diag_terms, "pcol", scatter_dimension=0, tiled=True),
    )
    sum_cross, sum_diag = lax.psum((part_cross, part_diag), "prow")
    second_parent_inverse = -sum_cross
    second_diagonal_inverse = (
        second_pivot_inverse
        - batched_left_t(second_scaled_factor, second_parent_inverse)
        - sum_diag
    )
    return (column_one, diag_one, column_two, second_parent_inverse, second_diagonal_inverse)


def solution(mesh):
    placed = (
        P("pcol", "prow"),
        P(),
        P(),
        P("pcol", "prow", None),
        P("pcol", None, None),
        P("pcol", "prow", None),
        P("pcol", None, None),
        P("pcol", None, None),
    )
    return jax.shard_map(
        body,
        mesh=mesh,
        in_specs=placed,
        out_specs=(
            P("prow", "pcol", None),
            P("pcol", None, None),
            P("prow", "pcol", None),
            P("pcol", None, None),
            P("pcol", None, None),
        ),
        check_vma=False,
    )
```

profile of v0, /device:TPU:9, one launch (start us, length us, event | category | flops | bytes accessed | tf_op | source)
XLA Modules:
  0.0 467.8 jit_solution(3958737760766188225)
XLA Ops:
  7.2 0.7 all-gather.4.cloned.1.call-update
  8.0 1.2 copy.34
  9.2 0.2 copy.35
  9.4 0.1 copy.33
  9.5 0.2 subtract_reduce_fusion.1
  9.7 0.7 gather_fusion.3
  10.5 28.8 %all-gather.4.cloned.1.call-done = f32[8,256,256]{2,1,0:T(8,128)} async-done(((f32[1,256,256]{2,1,0:T(8,128)}), f32[8,256,256]{2,1,0:T(8,128)}) %all-gather.4.cloned.1.call-update) | async-done | bytes 2097168 | tf_op jit(solution)/shard_map/all_gather | solution.py:45
  39.3 5.1 %fusion.2 = f32[8,256,256]{2,1,0:T(8,128)} fusion(f32[8,256,256]{2,1,0:T(8,128)} %all-gather.4.cloned.1.call-done, f32[8,256,256]{2,1,0:T(8,128)S(1)} %gather_fusion.3, pred[8]{0:T(512)(128)(4,1)S(1)} %compare_and_fusion.4), kind=kOutput, calls=%fused_computation.17 | convolution fusion | flops 1611137024 | bytes 6291464 | tf_op jit(solution)/shard_map/kab,kbd->kad/dot_general | solution.py:8
  44.4 0.7 all-gather.6.cloned.1.call-update
  45.2 0.5 all-gather.8.cloned.1.call-update
  45.7 0.2 compare_reduce_fusion.1
  45.9 1.0 sort.45
  46.9 0.6 gather_fusion.4
  47.6 1.7 gather_fusion.5
  49.3 79.4 %all-reduce.6.cloned.1.call-done = f32[8,256,256]{2,1,0:T(8,128)} async-done(((f32[8,256,256]{2,1,0:T(8,128)}), f32[8,256,256]{2,1,0:T(8,128)}) %all-reduce.6.cloned.1.call-update) | async-done | bytes 2097168 | tf_op jit(solution)/shard_map/psum | solution.py:58
  128.7 1.8 neg.9
  130.5 1.7 gather_fusion.6
  132.1 4.5 convolution_multiply_fusion.2
  136.6 0.2 broadcast.185.clone
  136.8 2.4 scatter_fusion
  139.2 1.3 copy-done.3
  140.6 0.6 gather_fusion
  141.2 0.1 broadcast_select_fusion
  141.3 0.2 subtract_reduce_fusion
  141.5 0.2 compare_reduce_fusion
  141.7 2.0 gather_fusion.7
  143.6 0.1 compare_and_fusion.6
  143.8 15.7 %all-gather.6.cloned.1.call-done = f32[8,256,256]{2,1,0:T(8,128)} async-done(((f32[1,256,256]{2,1,0:T(8,128)}), f32[8,256,256]{2,1,0:T(8,128)}) %all-gather.6.cloned.1.call-update) | async-done | bytes 2097168 | tf_op jit(solution)/shard_map/all_gather | solution.py:51
  159.4 5.8 %fusion = f32[8,256,256]{2,1,0:T(8,128)} fusion(f32[8,256,256]{2,1,0:T(8,128)} %all-gather.6.cloned.1.call-done, f32[8,256,256]{2,1,0:T(8,128)} %gather_fusion.7, pred[8]{0:T(512)(128)(4,1)S(1)} %compare_and_fusion.2), kind=kOutput, calls=%fused_computation.15 | convolution fusion | flops 1611137024 | bytes 6291464 | tf_op jit(solution)/shard_map/kab,kbd->kad/dot_general | solution.py:8
  165.2 0.6 gather_fusion.1
  165.8 23.2 %all-gather.8.cloned.1.call-done = f32[8,256,256]{2,1,0:T(8,128)} async-done(((f32[1,256,256]{2,1,0:T(8,128)}), f32[8,256,256]{2,1,0:T(8,128)}) %all-gather.8.cloned.1.call-update) | async-done | bytes 2097168 | tf_op jit(solution)/shard_map/all_gather | solution.py:52
  189.0 2.8 fusion.4
  191.7 40.9 %reduce-scatter.4.cloned.1.call-done = f32[1,256,256]{2,1,0:T(8,128)} async-done(((f32[8,256,256]{2,1,0:T(8,128)}), f32[1,256,256]{2,1,0:T(8,128)}) %reduce-scatter.4.cloned.1.call-update) | async-done | bytes 262160 | tf_op jit(solution)/shard_map/reduce_scatter | solution.py:73
  232.7 0.2 reduce-scatter.6.cloned.1.call-start
  232.9 1.0 sort.46
  233.9 0.6 gather_fusion.2
  234.5 0.6 gather_fusion.8
  235.2 1.0 sort.47
  236.3 0.6 dynamic-slice.18
  236.9 0.6 dynamic-slice.17
  238.7 0.7 and_reduce_fusion
  239.4 2.2 gather_fusion.10
  241.7 1.6 gather_fusion.9
  243.2 4.2 convolution_multiply_fusion.1
  247.5 0.2 broadcast.185.clone.1
  247.7 2.3 scatter_fusion.1
  250.0 78.2 %all-reduce.10.cloned.1.call-done = (f32[1,256,256]{2,1,0:T(8,128)}, f32[8,256,256]{2,1,0:T(8,128)}) async-done(((f32[1,256,256]{2,1,0:T(8,128)}, f32[8,256,256]{2,1,0:T(8,128)}), (f32[1,256,256]{2,1,0:T(8,128)}, f32[8,256,256]{2,1,0:T(8,128)})) %all-reduce.10.cloned.1.call-update) | async-done | bytes 2359312 | tf_op jit(solution)/shard_map/psum | solution.py:74
  328.2 1.1 sub.32
  329.3 2.0 fusion.8
  331.3 1.3 copy-done.1
  332.7 1.8 neg.10
  334.5 1.7 gather_fusion.11
  336.2 4.2 convolution_multiply_fusion
  340.4 0.2 broadcast.185.clone.2
  340.6 1.1 copy-done.8
  341.7 1.2 scatter_fusion.2
  342.9 1.3 copy-done.2
  344.3 30.1 %reduce-scatter.6.cloned.1.call-done = f32[1,256,256]{2,1,0:T(8,128)} async-done(((f32[8,256,256]{2,1,0:T(8,128)}), f32[1,256,256]{2,1,0:T(8,128)}) %reduce-scatter.6.cloned.1.call-update) | async-done | bytes 262160 | tf_op jit(solution)/shard_map/reduce_scatter | solution.py:99
  374.4 44.4 %reduce-scatter.8.cloned.1.call-done = f32[1,256,256]{2,1,0:T(8,128)} async-done(((f32[8,256,256]{2,1,0:T(8,128)}), f32[1,256,256]{2,1,0:T(8,128)}) %reduce-scatter.8.cloned.1.call-update) | async-done | bytes 262160 | tf_op jit(solution)/shard_map/reduce_scatter | solution.py:100
  418.9 1.9 constant_dynamic-slice_fusion.1
  420.8 1.9 constant_dynamic-slice_fusion
  422.6 35.3 %all-reduce.8.cloned.1.call-done = (f32[1,256,256]{2,1,0:T(8,128)}, f32[1,256,256]{2,1,0:T(8,128)}) async-done(((f32[1,256,256]{2,1,0:T(8,128)}, f32[1,256,256]{2,1,0:T(8,128)}), (f32[1,256,256]{2,1,0:T(8,128)}, f32[1,256,256]{2,1,0:T(8,128)})) %all-reduce.8.cloned.1.call-update) | async-done | bytes 524304 | tf_op jit(solution)/shard_map/psum | solution.py:102
  457.9 1.0 neg.11
  458.9 2.3 fusion.10
  (61 shorter events, 0.6 us)
Async XLA Ops:
  7.2 2.3 copy-start.13
  7.2 2.5 copy-start
  7.2 32.1 %all-gather.4.cloned.1.call-start = ((), (), s32[]{:S(2)}) async-start(), calls=%async_computation.3 | async-start | bytes 2359296 | tf_op jit(solution)/shard_map/all_gather | solution.py:45
  7.9 120.8 %all-reduce.6.cloned.1.call-start = ((), (), s32[]{:S(2)}) async-start(), calls=%async_computation.4 | async-start | bytes 4194304 | tf_op jit(solution)/shard_map/psum | solution.py:58
  44.3 3.2 copy-start.7
  44.4 115.0 %all-gather.6.cloned.1.call-start = ((), (), s32[]{:S(2)}) async-start(), calls=%async_computation.6 | async-start | bytes 2359296 | tf_op jit(solution)/shard_map/all_gather | solution.py:51
  45.1 143.9 %all-gather.8.cloned.1.call-start = ((), (), s32[]{:S(2)}) async-start(), calls=%async_computation.7 | async-start | bytes 2359296 | tf_op jit(solution)/shard_map/all_gather | solution.py:52
  45.7 187.0 %reduce-scatter.4.cloned.1.call-start = ((), (), s32[]{:S(2)}) async-start(), calls=%async_computation.5 | async-start | bytes 2359296 | tf_op jit(solution)/shard_map/reduce_scatter | solution.py:73
  130.5 1.7 copy-start.4
  139.2 1.3 copy-start.3
  140.6 187.7 %all-reduce.10.cloned.1.call-start = ((), (), s32[]{:S(2)}) async-start(), calls=%async_computation.11 | async-start | bytes 4718592 | tf_op jit(solution)/shard_map/psum | solution.py:74
  143.7 21.4 %copy-start.5 = (f32[8,256,256]{2,1,0:T(8,128)S(1)}, f32[8,256,256]{2,1,0:T(8,128)}, u32[]{:S(2)}) copy-start(f32[8,256,256]{2,1,0:T(8,128)} %copy-done.4) | copy-start | bytes 6291460
  191.7 47.0 %copy-start.14 = (s32[3]{0:T(128)S(1)}, s32[3]{0:T(128)}, u32[]{:S(2)}) copy-start(s32[3]{0:T(128)} %constant.171.clone.1) | copy-start | bytes 40
  232.7 141.8 %reduce-scatter.6.cloned.1.call-start = ((), (), s32[]{:S(2)}) async-start(), calls=%async_computation.8 | async-start | bytes 2359296 | tf_op jit(solution)/shard_map/reduce_scatter | solution.py:99
  329.3 5.2 %copy-start.9 = (f32[1,256,256]{2,1,0:T(8,128)}, f32[1,256,256]{2,1,0:T(8,128)S(1)}, u32[]{:S(2)}) copy-start(f32[1,256,256]{2,1,0:T(8,128)S(1)} %sub.32) | copy-start | bytes 786436
  331.3 1.3 copy-start.1
  332.7 86.2 %reduce-scatter.8.cloned.1.call-start = ((), (), s32[]{:S(2)}) async-start(), calls=%async_computation.9 | async-start | bytes 2359296 | tf_op jit(solution)/shard_map/reduce_scatter | solution.py:100
  334.5 1.7 copy-start.6
  340.4 1.3 copy-start.8
  342.9 1.3 copy-start.2
  344.2 114.6 %copy-start.10 = (f32[1,256,256]{2,1,0:T(8,128)S(1)}, f32[1,256,256]{2,1,0:T(8,128)}, u32[]{:S(2)}) copy-start(f32[1,256,256]{2,1,0:T(8,128)} %param.22) | copy-start | bytes 786436
  344.2 114.6 %copy-start.12 = (f32[1,256,256]{2,1,0:T(8,128)S(1)}, f32[1,256,256]{2,1,0:T(8,128)}, u32[]{:S(2)}) copy-start(f32[1,256,256]{2,1,0:T(8,128)} %param.23) | copy-start | bytes 786436
  344.3 113.6 %all-reduce.8.cloned.1.call-start = ((), (), s32[]{:S(2)}) async-start(), calls=%async_computation.10 | async-start | bytes 1048576 | tf_op jit(solution)/shard_map/psum | solution.py:102
  458.9 2.4 copy-start.11
Sparse Core Ops, SparseCore 0:
  9.9 29.3 all-gather.3
  44.5 84.1 all-reduce.5
  130.6 28.7 all-gather.5
  161.2 27.7 all-gather.7
  192.1 40.5 reduce-scatter.3
  235.0 93.2 all-reduce.9
  332.8 41.6 reduce-scatter.5
  377.7 41.0 reduce-scatter.7
  421.3 36.5 all-reduce.7
where the time goes:
time: 472 us; the launch traced here: 468 us
  waiting for transfers between devices  378 us (80%)
  matrix products  30.9 us (7%)
  local copies, waits for them, and re-layouts  26.6 us (6%)
  other arithmetic  16 us (3%)
  between operations  15.6 us (3%)
    psum x1, waiting for transfers between devices, body(): first_full = -lax.psum(first_terms, 'prow')  79.4 us
    psum x1, waiting for transfers between devices, body(): pivot_sum = lax.psum(pivot_part, 'prow')  78.2 us
    reduce_scatter x1, waiting for transfers between devices, body(): lax.psum_scatter(diag_terms, 'pcol', scatter_dimension=0, tiled=True)  44.4 us
    reduce_scatter x1, waiting for transfers between devices, body(): lax.psum_scatter(pivot_terms, 'pcol', scatter_dimension=0, tiled=True)  40.9 us
    psum x1, waiting for transfers between devices, body(): sum_cross, sum_diag = lax.psum((part_cross, part_diag), 'prow')  35.3 us
    reduce_scatter x1, waiting for transfers between devices, body(): lax.psum_scatter(cross_terms, 'pcol', scatter_dimension=0, tiled=True)  30.1 us
    all_gather x1, waiting for transfers between devices, body(): lowall = lax.all_gather(low_one, 'pcol', axis=0, tiled=True)  28.8 us
    all_gather x1, waiting for transfers between devices, body(): lax.all_gather(second_scaled_factor, 'pcol', axis=0, tiled=True)  23.2 us
  transfers between devices with their start and end apart: 9, of which 9 were waited for; matrix products, arithmetic and copies ran while one was open for 12% of the time, Pallas kernels for 0%

commit v1 on v0

v1 whole, which is shorter than its diff:
```python
import functools

import jax
import jax.numpy as jnp
from jax import lax
from jax.experimental import pallas as pl
from jax.experimental.pallas import tpu as pltpu
from jax.sharding import PartitionSpec as P

MESH = pl.DeviceIdType.MESH
CORES = 2


def split_dot(left, right, transposed):
    contract = (((0,), (0,)), ((), ())) if transposed else (((1,), (0,)), ((), ()))
    dot = functools.partial(
        lax.dot_general, dimension_numbers=contract, preferred_element_type=jnp.float32
    )
    left_hi, right_hi = left.astype(jnp.bfloat16), right.astype(jnp.bfloat16)
    left_lo = (left - left_hi.astype(jnp.float32)).astype(jnp.bfloat16)
    right_lo = (right - right_hi.astype(jnp.float32)).astype(jnp.bfloat16)
    return dot(left_hi, right_lo) + dot(left_lo, right_hi) + dot(left_hi, right_hi)


def product_kernel(transposed, masked, add, left_index, right_index, keep, left, right, *rest):
    out = rest[-1]
    value = split_dot(left[0], right[0], transposed)
    if masked:
        value = jnp.where(keep[pl.program_id(0)] > 0, value, 0.0)
    if add:
        value = rest[0][0] - value
    out[0] = value


def products(left, left_index, right, right_index, transposed=False, keep=None, minus_from=None):
    count = left_index.shape[0]
    width = left.shape[1]
    masked = keep is not None
    if keep is None:
        keep = left_index
    block = (1, width, width)
    specs = [
        pl.BlockSpec(block, lambda g, a, b, k: (a[g], 0, 0)),
        pl.BlockSpec(block, lambda g, a, b, k: (b[g], 0, 0)),
    ]
    args = [left, right]
    if minus_from is not None:
        specs.append(pl.BlockSpec(block, lambda g, a, b, k: (g, 0, 0)))
        args.append(minus_from)
    return pl.pallas_call(
        functools.partial(product_kernel, transposed, masked, minus_from is not None),
        out_shape=jax.ShapeDtypeStruct((count, width, width), jnp.float32),
        grid_spec=pltpu.PrefetchScalarGridSpec(
            num_scalar_prefetch=3,
            grid=(count,),
            in_specs=specs,
            out_specs=pl.BlockSpec(block, lambda g, a, b, k: (g, 0, 0)),
        ),
    )(left_index.astype(jnp.int32), right_index.astype(jnp.int32), keep.astype(jnp.int32), *args)


def exchange_kernel(kinds, rows, cols, *refs):
    count = len(kinds)
    sources, targets = refs[:count], refs[count : 2 * count]
    sems = refs[2 * count :]
    row, col = lax.axis_index("prow"), lax.axis_index("pcol")
    per = cols // rows
    chips = cols // CORES
    chip, core = col // CORES, lax.rem(col, CORES)
    partner = chip * CORES + (1 - core)
    own_place, home = lax.rem(col, per), col // per
    used = [axis for _, axis in kinds]

    barrier = pltpu.get_barrier_semaphore()
    expected = 0
    if "pcol" in used:
        for d in range(1, cols):
            pl.semaphore_signal(
                barrier, inc=1, device_id=(row, lax.rem(col + d, cols)), device_id_type=MESH
            )
        expected += cols - 1
    if "prow" in used:
        for d in range(1, rows):
            pl.semaphore_signal(
                barrier, inc=1, device_id=(lax.rem(row + d, rows), col), device_id_type=MESH
            )
        expected += rows - 1
    if "both" in used:
        for b in range(per):

            @pl.when(home != row)
            def _():
                pl.semaphore_signal(
                    barrier, inc=1, device_id=(home, row * per + b), device_id_type=MESH
                )

            if "pcol" not in used:

                @pl.when(jnp.logical_and(home == row, b != own_place))
                def _():
                    pl.semaphore_signal(
                        barrier, inc=1, device_id=(home, row * per + b), device_id_type=MESH
                    )

    if "both" in used:
        near = 0 if "pcol" in used else per - 1
        pl.semaphore_wait(barrier, expected + jnp.where(home != row, per, near))
    else:
        pl.semaphore_wait(barrier, expected)

    def remote(source, target, send, recv, device):
        return pltpu.make_async_remote_copy(
            src_ref=source,
            dst_ref=target,
            send_sem=send,
            recv_sem=recv,
            device_id=device,
            device_id_type=MESH,
        )

    copies, forwards, locals_ = [], [], []
    for op, (kind, axis) in enumerate(kinds):
        x, out = sources[op], targets[op]
        send, recv = sems[2 * op], sems[2 * op + 1]
        if kind == "transpose":
            continue
        size, me = (rows, row) if axis == "prow" else (cols, col)
        if kind == "gather" and axis == "pcol":
            for d in range(1, chips):
                there = lax.rem(chip + d, chips) * CORES + core
                copy = remote(x, out.at[me], send.at[d], recv.at[d], (row, there))
                copy.start()
                here = lax.rem(chip + chips - d, chips) * CORES + core
                forwards.append((copy, op, d, here))
            copy = remote(x, out.at[me], send.at[0], recv.at[0], (row, partner))
            copy.start()
            copies.append(copy)
        else:
            for d in range(1, size):
                there = lax.rem(me + d, size)
                device = (there, col) if axis == "prow" else (row, there)
                source = x if kind == "gather" else x.at[there]
                copy = remote(source, out.at[me], send.at[d], recv.at[d], device)
                copy.start()
                copies.append(copy)
        mine = x if kind == "gather" else x.at[me]
        local = pltpu.make_async_copy(mine, out.at[me], sems[2 * count].at[op])
        local.start()
        locals_.append(local)

    def away(op, b):
        return remote(
            sources[op],
            targets[op].at[own_place],
            sems[2 * op].at[b],
            sems[2 * op + 1].at[own_place],
            (home, row * per + b),
        )

    def near_copy(op, place):
        return pltpu.make_async_copy(
            sources[op], targets[op].at[place], sems[2 * op + 1].at[place]
        )

    def stays(b):
        return jnp.logical_and(home == row, b == own_place)

    transposes = [op for op, (kind, _) in enumerate(kinds) if kind == "transpose"]
    for op in transposes:
        for b in range(per):

            @pl.when(stays(b))
            def _():
                near_copy(op, own_place).start()

            @pl.when(jnp.logical_not(stays(b)))
            def _():
                away(op, b).start()

    for copy, op, d, here in forwards:
        copy.wait_recv()
        out = targets[op]
        forward = remote(
            out.at[here],
            out.at[here],
            sems[2 * op].at[chips - 1 + d],
            sems[2 * op + 1].at[chips - 1 + d],
            (row, partner),
        )
        forward.start()
        copies.append(forward)
    for copy, _, _, _ in forwards:
        copy.wait_send()
    for copy in copies:
        copy.wait_send()
        copy.wait_recv()
    for local in locals_:
        local.wait()
    for op in transposes:
        for b in range(per):

            @pl.when(jnp.logical_not(stays(b)))
            def _():
                away(op, b).wait_send()

        for a in range(per):
            near_copy(op, a).wait()


def exchange(number, *ops):
    rows, cols = lax.axis_size("prow"), lax.axis_size("pcol")
    shapes, scratch, kinds = [], [], []
    for kind, axis, x in ops:
        size = {"prow": rows, "pcol": cols, "both": cols // rows}[axis]
        lead = x.shape if kind != "all" else x.shape[1:]
        shapes.append(jax.ShapeDtypeStruct((size,) + lead, x.dtype))
        scratch += [pltpu.SemaphoreType.DMA((size,))] * 2
        kinds.append((kind, axis))
    scratch.append(pltpu.SemaphoreType.DMA((len(ops),)))
    anywhere = pl.BlockSpec(memory_space=pl.ANY)
    return pl.pallas_call(
        functools.partial(exchange_kernel, tuple(kinds), rows, cols),
        out_shape=shapes,
        in_specs=[anywhere] * len(ops),
        out_specs=[anywhere] * len(ops),
        scratch_shapes=scratch,
        compiler_params=pltpu.CompilerParams(collective_id=number, has_side_effects=True),
    )(*[x for _, _, x in ops])


def body(
    anc_inverse,
    pattern_one,
    parents,
    low_one,
    pivot_one,
    low_two,
    second_scaled_factor,
    second_pivot_inverse,
):
    row, col = lax.axis_index("prow"), lax.axis_index("pcol")
    rows, cols = lax.axis_size("prow"), lax.axis_size("pcol")
    per = cols // rows
    width = pivot_one.shape[1]
    piece = width // cols
    owned = anc_inverse.shape[1] // width
    zblocks = anc_inverse.reshape(width, owned, width).transpose(1, 0, 2)
    everyone = jnp.arange(cols, dtype=jnp.int32)
    mine = jnp.arange(per, dtype=jnp.int32)
    zero = jnp.zeros((1,), jnp.int32)
    place = col // per
    child = jnp.zeros((cols,), jnp.int32).at[parents].set(everyone)
    row_slots = lax.dynamic_index_in_dim(pattern_one, row, 1, keepdims=False) - row * owned
    row_slots_two = jnp.take(row_slots, parents)
    place_slots = lax.dynamic_index_in_dim(pattern_one, place, 1, keepdims=False)
    hit_one = lax.dynamic_slice_in_dim(place_slots, row * per, per) == col
    hit_two = lax.dynamic_slice_in_dim(jnp.take(place_slots, parents), row * per, per) == col
    one, two = low_one[0], low_two[0]

    def pieces(blocks):
        return blocks.reshape(per, cols, piece, width).transpose(1, 0, 2, 3)

    lowall, one_t, two_t, pivot_pieces = exchange(
        0,
        ("gather", "pcol", one),
        ("transpose", "both", one),
        ("transpose", "both", two),
        ("all", "pcol", pivot_one.reshape(cols, piece, width)),
    )
    parent_index = lax.dynamic_slice_in_dim(parents, col, 1)
    merged = products(lowall, parent_index, second_scaled_factor, zero, minus_from=low_two)[0]
    first_terms = products(zblocks, row_slots, lowall, everyone)
    mergedall, first_got = exchange(
        1,
        ("gather", "pcol", merged),
        ("all", "prow", first_terms.reshape(rows, per, width, width)),
    )
    column_one = -jnp.sum(first_got, axis=0)
    pivot_terms = products(one_t, mine, column_one, mine, transposed=True, keep=hit_one)
    second_terms = products(zblocks, row_slots_two, mergedall, everyone)
    of_child = lax.dynamic_index_in_dim(
        mergedall, lax.dynamic_index_in_dim(child, col, 0, keepdims=False), 0, keepdims=False
    )
    second_got, child_t, pivot_got = exchange(
        2,
        ("all", "prow", second_terms.reshape(rows, per, width, width)),
        ("transpose", "both", of_child),
        ("all", "pcol", pieces(pivot_terms)),
    )
    column_two = -jnp.sum(second_got, axis=0)
    pivot_piece = jnp.sum(pivot_got, axis=0)
    cross_terms = products(column_one, mine, child_t, mine, transposed=True, keep=hit_one)
    diag_terms = products(two_t, mine, column_two, mine, transposed=True, keep=hit_two)
    small_got, pivot_rows = exchange(
        3,
        ("all", "pcol", jnp.concatenate([pieces(cross_terms), pieces(diag_terms)], axis=1)),
        ("gather", "prow", pivot_piece),
    )
    pivot_rows = pivot_rows.reshape(cols, piece, width)
    small_rows, pivot_final = exchange(
        4,
        ("gather", "prow", jnp.sum(small_got, axis=0)),
        (
            "all",
            "pcol",
            jnp.stack(
                [
                    pivot_rows,
                    jnp.take(pivot_rows, parents, axis=0),
                    jnp.take(pivot_pieces, parents, axis=0),
                ],
                axis=1,
            ),
        ),
    )
    cross_rows = small_rows[:, :per].reshape(cols, piece, width)
    diag_rows = small_rows[:, per:].reshape(cols, piece, width)
    (small_final,) = exchange(
        5,
        ("all", "pcol", jnp.stack([jnp.take(cross_rows, parents, axis=0), diag_rows], axis=1)),
    )

    def whole(array, index):
        return array[:, index].reshape(1, width, width)

    diag_one = pivot_one - whole(pivot_final, 0)
    parent_sum = whole(pivot_final, 1)
    left = whole(pivot_final, 2) - parent_sum + parent_sum.transpose(0, 2, 1)
    second_parent_inverse = products(
        left, zero, second_scaled_factor, zero, minus_from=-whole(small_final, 0)
    )
    second_diagonal_inverse = products(
        second_scaled_factor,
        zero,
        second_parent_inverse,
        zero,
        transposed=True,
        minus_from=second_pivot_inverse - whole(small_final, 1),
    )
    return (column_one, diag_one, column_two, second_parent_inverse, second_diagonal_inverse)


def solution(mesh):
    placed = (
        P("pcol", "prow"),
        P(),
        P(),
        P("pcol", "prow", None),
        P("pcol", None, None),
        P("pcol", "prow", None),
        P("pcol", None, None),
        P("pcol", None, None),
    )
    return jax.shard_map(
        body,
        mesh=mesh,
        in_specs=placed,
        out_specs=(
            P("prow", "pcol", None),
            P("pcol", None, None),
            P("prow", "pcol", None),
            P("pcol", None, None),
            P("pcol", None, None),
        ),
        check_vma=False,
    )
```

time: 472 us -> 302 us (0.64)
  waiting for transfers between devices: 378 us -> 0 us
  Pallas kernels: 0 us -> 264 us
  matrix products: 30.9 us -> 0 us
  between operations: 15.6 us -> 2.83 us
  local copies, waits for them, and re-layouts: 26.6 us -> 16.6 us
    pallas_call x0 -> x14, Pallas kernels: none -> 264 us  [the longest x6 232 us: exchange(): pl.pallas_call(functools.partial(exchange_kernel, tuple(kinds), rows, col...]
    psum x3 -> x0, waiting for transfers between devices: 193 us -> none  [the longest x1 79.4 us: body(): first_full = -lax.psum(first_terms, 'prow')]
    reduce_scatter x3 -> x0, waiting for transfers between devices: 115 us -> none  [the longest x1 44.4 us: body(): lax.psum_scatter(diag_terms, 'pcol', scatter_dimension=0, tiled=True)]
    all_gather x3 -> x0, waiting for transfers between devices: 67.7 us -> none  [the longest x1 28.8 us: body(): lowall = lax.all_gather(low_one, 'pcol', axis=0, tiled=True)]
    dot_general x8 -> x0, matrix products: 30.9 us -> none  [the longest x4 15.6 us: batched(): jnp.einsum('kab,kbd->kad', left, right, precision=lax.Precision.HIGHEST)]
    gather x14 -> x5, local copies, waits for them, and re-layouts: 15.7 us -> 4.03 us  [the longest x1 1.61 us: body(): jnp.take(pivot_rows, parents, axis=0)]
    scatter-add x3 -> x0, other arithmetic: 5.85 us -> none  [the longest x1 2.36 us: body(): pivot_terms = jnp.zeros_like(first_full).at[rows_one].add(pivot_small)]
    unnamed x32 -> x21, local copies, waits for them, and re-layouts: 6.46 us -> 1.28 us
  transfers between devices with their start and end apart: 9 -> 0, of which waited for: 9 -> 0; matrix products, arithmetic and copies ran while one was open for 12% -> 0% of each run, Pallas kernels for 0% -> 0%
where the time goes in v1:
time: 302 us; the launch traced here: 301 us
  Pallas kernels  264 us (87%)
  other arithmetic  17.5 us (6%)
  local copies, waits for them, and re-layouts  16.6 us (5%)
    pallas_call x6, Pallas kernels, exchange(): pl.pallas_call(functools.partial(exchange_kernel, tuple(kinds), rows, col...  232 us
    pallas_call x8, Pallas kernels, products(): pl.pallas_call(functools.partial(product_kernel, transposed, masked, minu...  32 us

profile of v1, /device:TPU:9, one launch (start us, length us, event | category | flops | bytes accessed | tf_op | source)
XLA Modules:
  0.0 301.3 jit_solution(14112133048916357936)
XLA Ops:
  0.7 1.3 fusion.2
  1.9 70.9 %shard_map.119 = (f32[8,256,256]{2,1,0:T(8,128)}, f32[2,256,256]{2,1,0:T(8,128)}, f32[2,256,256]{2,1,0:T(8,128)}, f32[8,32,256]{2,1,0:T(8,128)}) custom-call(f32[256,256]{1,0:T(8,128)} %bitcast.64, f32[256,256]{1,0:T(8,128)} %bitcast.65, f32[256,256]{1,0:T(8,128)} %bitcast.56, f32[8,32,256]{2,1,0:T(8,128)} %bitcast.57), custom_call_target="tpu_custom_call" | custom-call | tf_op jit(solution)/shard_map/pallas_call | solution.py:221
  72.9 1.2 copy.16
  74.1 1.0 copy.17
  75.1 0.5 iota.20.right_index
  75.6 7.6 %shard_map.121 = f32[8,256,256]{2,1,0:T(8,128)} custom-call(s32[8]{0:T(128)} %get-tuple-element.43.left_index.keep, s32[8]{0:T(128)} %iota.20.right_index, s32[8]{0:T(128)} %get-tuple-element.43.left_index.keep, f32[2,256,256]{2,1,0:T(8,128)} %bitcast.46, f32[8,256,256]{2,1,0:T(8,128)} %get-tuple-element.20.left.right), custom_call_target="tpu_custom_call" | custom-call | tf_op jit(solution)/shard_map/pallas_call | solution.py:50
  83.2 0.0 copy-done.9
  83.2 0.6 dynamic_slice.24.left_index.keep
  83.8 3.4 %shard_map.120 = f32[1,256,256]{2,1,0:T(8,128)} custom-call(s32[1]{0:T(128)} %dynamic_slice.24.left_index.keep, s32[1]{0:T(128)} %constant.71.clone.1.right_index.left_index.keep, s32[1]{0:T(128)} %dynamic_slice.24.left_index.keep, f32[8,256,256]{2,1,0:T(8,128)} %get-tuple-element.20.left.right, f32[1,256,256]{2,1,0:T(8,128)} %left.1, f32[1,256,256]{2,1,0:T(8,128)} %rest_0_.1), custom_call_target="tpu_custom_call" | custom-call | tf_op jit(solution)/shard_map/pallas_call | solution.py:50
  87.2 49.8 %shard_map.122 = (f32[8,256,256]{2,1,0:T(8,128)}, f32[4,2,256,256]{3,2,1,0:T(8,128)}) custom-call(f32[256,256]{1,0:T(8,128)} %bitcast.55, f32[4,2,256,256]{3,2,1,0:T(8,128)} %bitcast.45), custom_call_target="tpu_custom_call" | custom-call | tf_op jit(solution)/shard_map/pallas_call | solution.py:221
  137.0 1.8 reduce_sum.36
  138.8 0.0 copy-start
  138.8 0.8 neg.11.right.left
  139.6 1.3 fusion.3.keep
  140.9 0.5 iota.24.left_index.right_index
  141.4 3.1 %shard_map.124 = f32[2,256,256]{2,1,0:T(8,128)} custom-call(s32[2]{0:T(128)} %iota.24.left_index.right_index, s32[2]{0:T(128)} %iota.24.left_index.right_index, s32[2]{0:T(128)} %fusion.3.keep, f32[2,256,256]{2,1,0:T(8,128)} %get-tuple-element.23.left, f32[2,256,256]{2,1,0:T(8,128)} %neg.11.right.left), custom_call_target="tpu_custom_call" | custom-call | tf_op jit(solution)/shard_map/pallas_call | solution.py:50
  144.5 1.9 copy.25
  146.4 0.0 copy-done
  146.4 0.6 gather_fusion
  147.1 0.5 broadcast_select_fusion.1
  147.6 0.5 iota.22.right_index
  148.1 7.5 %shard_map.123 = f32[8,256,256]{2,1,0:T(8,128)} custom-call(s32[8]{0:T(128)} %get-tuple-element.33.left_index.keep, s32[8]{0:T(128)} %iota.22.right_index, s32[8]{0:T(128)} %get-tuple-element.33.left_index.keep, f32[2,256,256]{2,1,0:T(8,128)} %bitcast.47, f32[8,256,256]{2,1,0:T(8,128)} %get-tuple-element.22.right), custom_call_target="tpu_custom_call" | custom-call | tf_op jit(solution)/shard_map/pallas_call | solution.py:50
  155.6 0.6 scatter_custom_fusion
  156.2 0.6 dynamic_slice.27
  158.7 1.7 dynamic-slice_bitcast_fusion.refs_1_
  160.4 59.2 %shard_map.125 = (f32[4,2,256,256]{3,2,1,0:T(8,128)}, f32[2,256,256]{2,1,0:T(8,128)}, f32[8,2,32,256]{3,2,1,0:T(8,128)}) custom-call(f32[4,2,256,256]{3,2,1,0:T(8,128)} %bitcast.44, f32[256,256]{1,0:T(8,128)} %dynamic-slice_bitcast_fusion.refs_1_, f32[8,2,32,256]{3,2,1,0:T(8,128)} %bitcast.54), custom_call_target="tpu_custom_call" | custom-call | tf_op jit(solution)/shard_map/pallas_call | solution.py:221
  219.6 0.5 iota.21.left_index.right_index
  220.1 3.1 %shard_map.126 = f32[2,256,256]{2,1,0:T(8,128)} custom-call(s32[2]{0:T(128)} %iota.21.left_index.right_index, s32[2]{0:T(128)} %iota.21.left_index.right_index, s32[2]{0:T(128)} %fusion.3.keep, f32[2,256,256]{2,1,0:T(8,128)} %neg.11.right.left, f32[2,256,256]{2,1,0:T(8,128)} %get-tuple-element.24.right), custom_call_target="tpu_custom_call" | custom-call | tf_op jit(solution)/shard_map/pallas_call | solution.py:50
  223.2 1.8 reduce_sum.37
  225.0 0.0 copy-start.1
  225.0 0.8 neg.12.right
  225.9 0.6 gather_fusion.1
  226.5 0.6 compare_convert_fusion.keep
  227.1 0.5 iota.25.left_index.right_index
  227.6 3.1 %shard_map.127 = f32[2,256,256]{2,1,0:T(8,128)} custom-call(s32[2]{0:T(128)} %iota.25.left_index.right_index, s32[2]{0:T(128)} %iota.25.left_index.right_index, s32[2]{0:T(128)} %compare_convert_fusion.keep, f32[2,256,256]{2,1,0:T(8,128)} %get-tuple-element.25.left, f32[2,256,256]{2,1,0:T(8,128)} %neg.12.right), custom_call_target="tpu_custom_call" | custom-call | tf_op jit(solution)/shard_map/pallas_call | solution.py:50
  230.8 1.2 copy_bitcast_fusion
  231.9 1.1 pad_maximum_fusion.refs_0_
  233.0 0.7 reduce_sum.38.refs_1_
  233.7 28.2 %shard_map.128 = (f32[8,4,32,256]{3,2,1,0:T(8,128)}, f32[4,2,32,256]{3,2,1,0:T(8,128)}) custom-call(f32[8,4,32,256]{3,2,1,0:T(8,128)} %pad_maximum_fusion.refs_0_, f32[2,32,256]{2,1,0:T(8,128)} %reduce_sum.38.refs_1_), custom_call_target="tpu_custom_call" | custom-call | tf_op jit(solution)/shard_map/pallas_call | solution.py:221
  261.9 0.0 copy-start.4
  261.9 0.0 copy-start.2
  261.9 1.6 gather_fusion.2
  263.6 0.6 gather_fusion.3
  264.1 0.1 select_bitcast_fusion.2
  264.2 0.0 copy-done.4
  264.2 1.0 pad_maximum_fusion.1.refs_1_
  265.2 0.0 copy-done.2
  265.2 0.7 reduce_sum.39.refs_0_
  265.9 14.0 %shard_map.129 = (f32[4,4,32,256]{3,2,1,0:T(8,128)}, f32[8,3,32,256]{3,2,1,0:T(8,128)}) custom-call(f32[4,32,256]{2,1,0:T(8,128)} %reduce_sum.39.refs_0_, f32[8,3,32,256]{3,2,1,0:T(8,128)} %pad_maximum_fusion.1.refs_1_), custom_call_target="tpu_custom_call" | custom-call | tf_op jit(solution)/shard_map/pallas_call | solution.py:221
  280.0 1.1 fusion.8
  281.1 0.6 gather_fusion.4
  281.7 0.1 select_bitcast_fusion
  281.8 0.9 pad_maximum_fusion.2.refs_0_
  282.6 10.3 %shard_map.130 = f32[8,2,32,256]{3,2,1,0:T(8,128)} custom-call(f32[8,2,32,256]{3,2,1,0:T(8,128)} %pad_maximum_fusion.2.refs_0_), custom_call_target="tpu_custom_call" | custom-call | tf_op jit(solution)/shard_map/pallas_call | solution.py:221
  292.9 1.8 fusion.7
  294.7 0.0 copy-done.5
  294.7 0.1 fusion.6
  294.7 0.1 copy.21
  294.9 0.0 copy-start.3
  294.9 0.8 bitcast_add_fusion.left
  295.6 2.1 shard_map.131.right
  297.7 0.7 sub.35.rest_0_
  298.5 2.1 shard_map.132
  300.6 0.7 sub.33
  (14 shorter events, 0.0 us)
Async XLA Ops:
  75.6 7.6 %copy-start.9 = (s32[8]{0:T(128)S(1)}, s32[8]{0:T(128)}, u32[]{:S(2)}) copy-start(s32[8]{0:T(128)} %param.14) | copy-start | bytes 100
  138.8 7.6 %copy-start = (s32[8]{0:T(128)S(1)}, s32[8]{0:T(128)}, u32[]{:S(2)}) copy-start(s32[8]{0:T(128)} %get-tuple-element.43.left_index.keep) | copy-start | bytes 100
  225.0 5.7 %copy-start.1 = (f32[2,256,256]{2,1,0:T(8,128)S(1)}, f32[2,256,256]{2,1,0:T(8,128)}, u32[]{:S(2)}) copy-start(f32[2,256,256]{2,1,0:T(8,128)} %shard_map.126) | copy-start | bytes 1572868
  230.8 2.3 copy-start.6
  231.9 31.6 %copy-start.8 = (f32[8,32,256]{2,1,0:T(8,128)S(1)}, f32[8,32,256]{2,1,0:T(8,128)}, u32[]{:S(2)}) copy-start(f32[8,32,256]{2,1,0:T(8,128)} %get-tuple-element.30) | copy-start | bytes 786436
  261.9 2.3 copy-start.4
  261.9 3.3 %copy-start.2 = (f32[8,4,32,256]{3,2,1,0:T(8,128)S(1)}, f32[8,4,32,256]{3,2,1,0:T(8,128)}, u32[]{:S(2)}) copy-start(f32[8,4,32,256]{3,2,1,0:T(8,128)} %get-tuple-element.28) | copy-start | bytes 3145732
  281.1 13.6 %copy-start.5 = (f32[8,3,32,256]{3,2,1,0:T(8,128)S(1)}, f32[8,3,32,256]{3,2,1,0:T(8,128)}, u32[]{:S(2)}) copy-start(f32[8,3,32,256]{3,2,1,0:T(8,128)} %get-tuple-element.31) | copy-start | bytes 2359300
  294.7 3.1 %copy-start.7 = (f32[1,256,256]{2,1,0:T(8,128)S(1)}, f32[1,256,256]{2,1,0:T(8,128)}, u32[]{:S(2)}) copy-start(f32[1,256,256]{2,1,0:T(8,128)} %param.19) | copy-start | bytes 786436
  294.9 5.7 %copy-start.3 = (f32[1,256,256]{2,1,0:T(8,128)S(1)}, f32[1,256,256]{2,1,0:T(8,128)}, u32[]{:S(2)}) copy-start(f32[1,256,256]{2,1,0:T(8,128)} %param.16) | copy-start | bytes 786436

commit v2 on v1

--- a/solution.py
+++ b/solution.py
@@ -22,41 +22,52 @@
     return dot(left_hi, right_lo) + dot(left_lo, right_hi) + dot(left_hi, right_hi)
 
 
-def product_kernel(transposed, masked, add, left_index, right_index, keep, left, right, *rest):
-    out = rest[-1]
+def product_kernel(transposed, keep_at, negate, prefetched, *refs):
+    left, right, out = refs[prefetched], refs[prefetched + 1], refs[-1]
     value = split_dot(left[0], right[0], transposed)
-    if masked:
-        value = jnp.where(keep[pl.program_id(0)] > 0, value, 0.0)
-    if add:
-        value = rest[0][0] - value
+    if keep_at is not None:
+        value = jnp.where(refs[keep_at][pl.program_id(0)] > 0, value, 0.0)
+    if len(refs) > prefetched + 3:
+        value = refs[prefetched + 2][0] - value
+    elif negate:
+        value = -value
     out[0] = value
 
 
-def products(left, left_index, right, right_index, transposed=False, keep=None, minus_from=None):
-    count = left_index.shape[0]
+def products(
+    count, left, right, left_index=None, right_index=None, transposed=False, keep=None,
+    minus_from=None, negate=False,
+):
     width = left.shape[1]
-    masked = keep is not None
-    if keep is None:
-        keep = left_index
     block = (1, width, width)
-    specs = [
-        pl.BlockSpec(block, lambda g, a, b, k: (a[g], 0, 0)),
-        pl.BlockSpec(block, lambda g, a, b, k: (b[g], 0, 0)),
-    ]
+    prefetch = []
+
+    def chosen(index):
+        if index is None:
+            return pl.BlockSpec(block, lambda g, *p: (g, 0, 0))
+        at = len(prefetch)
+        prefetch.append(index.astype(jnp.int32))
+        return pl.BlockSpec(block, lambda g, *p: (p[at][g], 0, 0))
+
+    specs = [chosen(left_index), chosen(right_index)]
     args = [left, right]
     if minus_from is not None:
-        specs.append(pl.BlockSpec(block, lambda g, a, b, k: (g, 0, 0)))
+        specs.append(chosen(None))
         args.append(minus_from)
+    keep_at = None
+    if keep is not None:
+        keep_at = len(prefetch)
+        prefetch.append(keep.astype(jnp.int32))
     return pl.pallas_call(
-        functools.partial(product_kernel, transposed, masked, minus_from is not None),
+        functools.partial(product_kernel, transposed, keep_at, negate, len(prefetch)),
         out_shape=jax.ShapeDtypeStruct((count, width, width), jnp.float32),
         grid_spec=pltpu.PrefetchScalarGridSpec(
-            num_scalar_prefetch=3,
+            num_scalar_prefetch=len(prefetch),
             grid=(count,),
             in_specs=specs,
-            out_specs=pl.BlockSpec(block, lambda g, a, b, k: (g, 0, 0)),
+            out_specs=chosen(None),
         ),
-    )(left_index.astype(jnp.int32), right_index.astype(jnp.int32), keep.astype(jnp.int32), *args)
+    )(*prefetch, *args)
 
 
 def exchange_kernel(kinds, rows, cols, *refs):
@@ -86,27 +97,15 @@
             )
         expected += rows - 1
     if "both" in used:
-        for b in range(per):
-
-            @pl.when(home != row)
-            def _():
-                pl.semaphore_signal(
-                    barrier, inc=1, device_id=(home, row * per + b), device_id_type=MESH
-                )
-
-            if "pcol" not in used:
-
-                @pl.when(jnp.logical_and(home == row, b != own_place))
-                def _():
-                    pl.semaphore_signal(
-                        barrier, inc=1, device_id=(home, row * per + b), device_id_type=MESH
-                    )
-
-    if "both" in used:
-        near = 0 if "pcol" in used else per - 1
-        pl.semaphore_wait(barrier, expected + jnp.where(home != row, per, near))
-    else:
-        pl.semaphore_wait(barrier, expected)
+
+        @pl.when(home != row)
+        def _():
+            pl.semaphore_signal(
+                barrier, inc=1, device_id=(home, row * per + own_place), device_id_type=MESH
+            )
+
+        expected += jnp.where(home != row, 1, 0)
+    pl.semaphore_wait(barrier, expected)
 
     def remote(source, target, send, recv, device):
         return pltpu.make_async_remote_copy(
@@ -148,34 +147,30 @@
         local.start()
         locals_.append(local)
 
-    def away(op, b):
+    def away(op):
         return remote(
             sources[op],
             targets[op].at[own_place],
-            sems[2 * op].at[b],
-            sems[2 * op + 1].at[own_place],
-            (home, row * per + b),
+            sems[2 * op].at[0],
+            sems[2 * op + 1].at[0],
+            (home, row * per + own_place),
         )
 
-    def near_copy(op, place):
+    def near(op):
         return pltpu.make_async_copy(
-            sources[op], targets[op].at[place], sems[2 * op + 1].at[place]
+            sources[op], targets[op].at[own_place], sems[2 * op + 1].at[0]
         )
-
-    def stays(b):
-        return jnp.logical_and(home == row, b == own_place)
 
     transposes = [op for op, (kind, _) in enumerate(kinds) if kind == "transpose"]
     for op in transposes:
-        for b in range(per):
-
-            @pl.when(stays(b))
-            def _():
-                near_copy(op, own_place).start()
-
-            @pl.when(jnp.logical_not(stays(b)))
-            def _():
-                away(op, b).start()
+
+        @pl.when(home == row)
+        def _():
+            near(op).start()
+
+        @pl.when(home != row)
+        def _():
+            away(op).start()
 
     for copy, op, d, here in forwards:
         copy.wait_recv()
@@ -189,6 +184,25 @@
         )
         forward.start()
         copies.append(forward)
+    for op in transposes:
+        near(op).wait()
+
+        @pl.when(home != row)
+        def _():
+            away(op).wait_send()
+
+        out = targets[op]
+        for d in range(1, per):
+            there = home * per + lax.rem(own_place + d, per)
+            forward = remote(
+                out.at[own_place],
+                out.at[own_place],
+                sems[2 * op].at[d],
+                sems[2 * op + 1].at[d],
+                (row, there),
+            )
+            forward.start()
+            copies.append(forward)
     for copy, _, _, _ in forwards:
         copy.wait_send()
     for copy in copies:
@@ -196,17 +210,6 @@
         copy.wait_recv()
     for local in locals_:
         local.wait()
-    for op in transposes:
-        for b in range(per):
-
-            @pl.when(jnp.logical_not(stays(b)))
-            def _():
-                away(op, b).wait_send()
-
-        for a in range(per):
-            near_copy(op, a).wait()
-
-
 def exchange(number, *ops):
     rows, cols = lax.axis_size("prow"), lax.axis_size("pcol")
     shapes, scratch, kinds = [], [], []
@@ -246,8 +249,6 @@
     owned = anc_inverse.shape[1] // width
     zblocks = anc_inverse.reshape(width, owned, width).transpose(1, 0, 2)
     everyone = jnp.arange(cols, dtype=jnp.int32)
-    mine = jnp.arange(per, dtype=jnp.int32)
-    zero = jnp.zeros((1,), jnp.int32)
     place = col // per
     child = jnp.zeros((cols,), jnp.int32).at[parents].set(everyone)
     row_slots = lax.dynamic_index_in_dim(pattern_one, row, 1, keepdims=False) - row * owned
@@ -260,24 +261,29 @@
     def pieces(blocks):
         return blocks.reshape(per, cols, piece, width).transpose(1, 0, 2, 3)
 
-    lowall, one_t, two_t, pivot_pieces = exchange(
+    lowall, one_t, pivot_pieces = exchange(
         0,
         ("gather", "pcol", one),
         ("transpose", "both", one),
-        ("transpose", "both", two),
         ("all", "pcol", pivot_one.reshape(cols, piece, width)),
     )
     parent_index = lax.dynamic_slice_in_dim(parents, col, 1)
-    merged = products(lowall, parent_index, second_scaled_factor, zero, minus_from=low_two)[0]
-    first_terms = products(zblocks, row_slots, lowall, everyone)
-    mergedall, first_got = exchange(
+    merged = products(
+        1, lowall, second_scaled_factor, left_index=parent_index, minus_from=low_two
+    )[0]
+    first_terms = products(cols, zblocks, lowall, left_index=row_slots, negate=True)
+    mergedall, first_got, two_t, pivot_parent = exchange(
         1,
         ("gather", "pcol", merged),
         ("all", "prow", first_terms.reshape(rows, per, width, width)),
-    )
-    column_one = -jnp.sum(first_got, axis=0)
-    pivot_terms = products(one_t, mine, column_one, mine, transposed=True, keep=hit_one)
-    second_terms = products(zblocks, row_slots_two, mergedall, everyone)
+        ("transpose", "both", two),
+        ("all", "pcol", jnp.take(pivot_pieces, parents, axis=0)),
+    )
+    column_one = jnp.sum(first_got, axis=0)
+    pivot_terms = products(per, one_t, column_one, transposed=True, keep=hit_one)
+    second_terms = products(
+        cols, zblocks, mergedall, left_index=row_slots_two, negate=True
+    )
     of_child = lax.dynamic_index_in_dim(
         mergedall, lax.dynamic_index_in_dim(child, col, 0, keepdims=False), 0, keepdims=False
     )
@@ -287,10 +293,10 @@
         ("transpose", "both", of_child),
         ("all", "pcol", pieces(pivot_terms)),
     )
-    column_two = -jnp.sum(second_got, axis=0)
+    column_two = jnp.sum(second_got, axis=0)
     pivot_piece = jnp.sum(pivot_got, axis=0)
-    cross_terms = products(column_one, mine, child_t, mine, transposed=True, keep=hit_one)
-    diag_terms = products(two_t, mine, column_two, mine, transposed=True, keep=hit_two)
+    cross_terms = products(per, column_one, child_t, transposed=True, keep=hit_one)
+    diag_terms = products(per, two_t, column_two, transposed=True, keep=hit_two)
     small_got, pivot_rows = exchange(
         3,
         ("all", "pcol", jnp.concatenate([pieces(cross_terms), pieces(diag_terms)], axis=1)),
@@ -303,14 +309,7 @@
         (
             "all",
             "pcol",
-            jnp.stack(
-                [
-                    pivot_rows,
-                    jnp.take(pivot_rows, parents, axis=0),
-                    jnp.take(pivot_pieces, parents, axis=0),
-                ],
-                axis=1,
-            ),
+            jnp.stack([pivot_rows, jnp.take(pivot_rows, parents, axis=0)], axis=1),
         ),
     )
     cross_rows = small_rows[:, :per].reshape(cols, piece, width)
@@ -325,15 +324,14 @@
 
     diag_one = pivot_one - whole(pivot_final, 0)
     parent_sum = whole(pivot_final, 1)
-    left = whole(pivot_final, 2) - parent_sum + parent_sum.transpose(0, 2, 1)
+    left = pivot_parent.reshape(1, width, width) - parent_sum + parent_sum.transpose(0, 2, 1)
     second_parent_inverse = products(
-        left, zero, second_scaled_factor, zero, minus_from=-whole(small_final, 0)
+        1, left, second_scaled_factor, minus_from=-whole(small_final, 0)
     )
     second_diagonal_inverse = products(
+        1,
         second_scaled_factor,
-        zero,
         second_parent_inverse,
-        zero,
         transposed=True,
         minus_from=second_pivot_inverse - whole(small_final, 1),
     )

time: 302 us -> 266 us (0.88)
  Pallas kernels: 264 us -> 227 us
    pallas_call x6, Pallas kernels: 232 us -> 196 us  [exchange(): pl.pallas_call(functools.partial(exchange_kernel, tuple(kinds), rows, col...]
where the time goes in v2:
time: 266 us; the launch traced here: 265 us
  Pallas kernels  227 us (85%)
  other arithmetic  19.5 us (7%)
  local copies, waits for them, and re-layouts  15.6 us (6%)
  between operations  2.83 us (1%)
    pallas_call x6, Pallas kernels, exchange(): pl.pallas_call(functools.partial(exchange_kernel, tuple(kinds), rows, col...  196 us
    pallas_call x8, Pallas kernels, products(): pl.pallas_call(functools.partial(product_kernel, transposed, keep_at, neg...  31.4 us

profile of v2, /device:TPU:9, one launch (start us, length us, event | category | flops | bytes accessed | tf_op | source)
XLA Modules:
  0.0 265.2 jit_solution(1754620364775697352)
XLA Ops:
  0.7 1.2 dynamic_slice.24.refs_0_
  1.9 1.3 fusion.3.refs_0_
  3.2 0.8 fusion.2
  4.0 0.0 copy-start
  4.0 0.7 compare_select_fusion
  4.7 0.6 scatter_custom_fusion
  5.3 0.6 dynamic_slice.27
  7.8 0.6 gather_fusion.2
  8.5 0.6 gather_fusion.1
  9.1 1.3 broadcast_select_fusion.2
  10.4 0.6 compare_convert_fusion.refs_0_
  10.9 1.2 copy.16
  12.2 1.0 copy.17
  13.2 30.0 %shard_map.119 = (f32[8,256,256]{2,1,0:T(8,128)}, f32[2,256,256]{2,1,0:T(8,128)}, f32[8,32,256]{2,1,0:T(8,128)}) custom-call(f32[256,256]{1,0:T(8,128)} %bitcast.58, f32[256,256]{1,0:T(8,128)} %bitcast.59, f32[8,32,256]{2,1,0:T(8,128)} %bitcast.60), custom_call_target="tpu_custom_call" | custom-call | tf_op jit(solution)/shard_map/pallas_call | solution.py:224
  43.1 1.5 gather_fusion
  44.7 0.0 copy-done
  44.7 0.8 broadcast_select_fusion.refs_3_
  45.5 2.7 %shard_map.120 = f32[1,256,256]{2,1,0:T(8,128)} custom-call(s32[1]{0:T(128)} %dynamic_slice.24.refs_0_, f32[8,256,256]{2,1,0:T(8,128)} %get-tuple-element.21.refs_1_.refs_2_, f32[1,256,256]{2,1,0:T(8,128)} %refs_0_.1, f32[1,256,256]{2,1,0:T(8,128)} %refs_3_.1), custom_call_target="tpu_custom_call" | custom-call | tf_op jit(solution)/shard_map/pallas_call | solution.py:61
  48.2 7.6 %shard_map.121 = f32[8,256,256]{2,1,0:T(8,128)} custom-call(s32[8]{0:T(128)} %copy-done, f32[2,256,256]{2,1,0:T(8,128)} %bitcast.49, f32[8,256,256]{2,1,0:T(8,128)} %get-tuple-element.21.refs_1_.refs_2_), custom_call_target="tpu_custom_call" | custom-call | tf_op jit(solution)/shard_map/pallas_call | solution.py:61
  55.8 54.8 %shard_map.122 = (f32[8,256,256]{2,1,0:T(8,128)}, f32[4,2,256,256]{3,2,1,0:T(8,128)}, f32[2,256,256]{2,1,0:T(8,128)}, f32[8,32,256]{2,1,0:T(8,128)}) custom-call(f32[256,256]{1,0:T(8,128)} %bitcast.67, f32[4,2,256,256]{3,2,1,0:T(8,128)} %bitcast.47, f32[256,256]{1,0:T(8,128)} %bitcast.66, f32[8,32,256]{2,1,0:T(8,128)} %broadcast_select_fusion.refs_3_), custom_call_target="tpu_custom_call" | custom-call | tf_op jit(solution)/shard_map/pallas_call | solution.py:224
  110.5 2.6 reduce_sum.36.refs_2_.refs_1_
  113.1 3.1 %shard_map.124 = f32[2,256,256]{2,1,0:T(8,128)} custom-call(s32[2]{0:T(128)} %fusion.3.refs_0_, f32[2,256,256]{2,1,0:T(8,128)} %get-tuple-element.25.refs_1_, f32[2,256,256]{2,1,0:T(8,128)} %reduce_sum.36.refs_2_.refs_1_), custom_call_target="tpu_custom_call" | custom-call | tf_op jit(solution)/shard_map/pallas_call | solution.py:61
  116.2 1.9 copy.25
  118.1 1.7 dynamic-slice_bitcast_fusion.refs_1_
  119.8 7.6 %shard_map.123 = f32[8,256,256]{2,1,0:T(8,128)} custom-call(s32[8]{0:T(128)} %get-tuple-element.35.refs_0_, f32[2,256,256]{2,1,0:T(8,128)} %bitcast.50, f32[8,256,256]{2,1,0:T(8,128)} %get-tuple-element.24.refs_2_), custom_call_target="tpu_custom_call" | custom-call | tf_op jit(solution)/shard_map/pallas_call | solution.py:61
  127.3 62.3 %shard_map.125 = (f32[4,2,256,256]{3,2,1,0:T(8,128)}, f32[2,256,256]{2,1,0:T(8,128)}, f32[8,2,32,256]{3,2,1,0:T(8,128)}) custom-call(f32[4,2,256,256]{3,2,1,0:T(8,128)} %bitcast.48, f32[256,256]{1,0:T(8,128)} %dynamic-slice_bitcast_fusion.refs_1_, f32[8,2,32,256]{3,2,1,0:T(8,128)} %bitcast.56), custom_call_target="tpu_custom_call" | custom-call | tf_op jit(solution)/shard_map/pallas_call | solution.py:224
  189.7 0.0 copy-start.1
  189.7 3.2 %shard_map.126 = f32[2,256,256]{2,1,0:T(8,128)} custom-call(s32[2]{0:T(128)} %fusion.3.refs_0_, f32[2,256,256]{2,1,0:T(8,128)} %reduce_sum.36.refs_2_.refs_1_, f32[2,256,256]{2,1,0:T(8,128)} %get-tuple-element.26.refs_2_), custom_call_target="tpu_custom_call" | custom-call | tf_op jit(solution)/shard_map/pallas_call | solution.py:61
  192.9 1.7 reduce_sum.38.refs_1_
  194.6 0.0 copy-done.1
  194.6 0.0 copy-start.2
  194.6 1.0 reduce_sum.37.refs_2_
  195.5 3.0 %shard_map.127 = f32[2,256,256]{2,1,0:T(8,128)} custom-call(s32[2]{0:T(128)} %compare_convert_fusion.refs_0_, f32[2,256,256]{2,1,0:T(8,128)} %get-tuple-element.27.refs_1_, f32[2,256,256]{2,1,0:T(8,128)} %reduce_sum.37.refs_2_), custom_call_target="tpu_custom_call" | custom-call | tf_op jit(solution)/shard_map/pallas_call | solution.py:61
  198.6 0.0 copy-done.2
  198.6 1.1 copy_bitcast_fusion
  199.7 1.1 pad_maximum_fusion.refs_0_
  200.8 24.4 %shard_map.128 = (f32[8,4,32,256]{3,2,1,0:T(8,128)}, f32[4,2,32,256]{3,2,1,0:T(8,128)}) custom-call(f32[8,4,32,256]{3,2,1,0:T(8,128)} %pad_maximum_fusion.refs_0_, f32[2,32,256]{2,1,0:T(8,128)} %reduce_sum.38.refs_1_), custom_call_target="tpu_custom_call" | custom-call | tf_op jit(solution)/shard_map/pallas_call | solution.py:224
  225.2 0.0 copy-start.4
  225.2 2.0 reduce_sum.39.refs_0_
  227.2 0.0 copy-start.3
  227.2 1.6 gather_fusion.3
  228.7 0.1 select_bitcast_fusion.1
  228.8 0.0 copy-done.4
  228.8 0.0 copy-start.7
  228.8 0.8 pad_maximum_fusion.1.refs_1_
  229.7 15.0 %shard_map.129 = (f32[4,4,32,256]{3,2,1,0:T(8,128)}, f32[8,2,32,256]{3,2,1,0:T(8,128)}) custom-call(f32[4,32,256]{2,1,0:T(8,128)} %reduce_sum.39.refs_0_, f32[8,2,32,256]{3,2,1,0:T(8,128)} %pad_maximum_fusion.1.refs_1_), custom_call_target="tpu_custom_call" | custom-call | tf_op jit(solution)/shard_map/pallas_call | solution.py:224
  244.6 0.0 copy-start.5
  244.7 1.1 fusion.8
  245.8 0.0 copy-done.3
  245.8 0.7 sub.33
  246.5 0.1 copy.21
  246.7 0.0 copy-done.7
  246.7 0.8 bitcast_add_fusion.refs_0_
  247.4 0.0 copy-done.5
  247.5 0.0 copy-start.6
  247.5 0.6 gather_fusion.4
  248.1 0.1 select_bitcast_fusion
  248.2 0.8 pad_maximum_fusion.2.refs_0_
  249.0 9.4 %shard_map.130 = f32[8,2,32,256]{3,2,1,0:T(8,128)} custom-call(f32[8,2,32,256]{3,2,1,0:T(8,128)} %pad_maximum_fusion.2.refs_0_), custom_call_target="tpu_custom_call" | custom-call | tf_op jit(solution)/shard_map/pallas_call | solution.py:224
  258.4 1.8 fusion.6
  260.2 0.0 copy-done.6
  260.2 0.7 sub.35.refs_2_
  260.9 2.1 shard_map.131.refs_1_
  263.0 2.1 shard_map.132
  (4 shorter events, 0.1 us)
Async XLA Ops:
  4.0 40.7 %copy-start = (s32[8]{0:T(128)}, s32[8]{0:T(128)S(1)}, u32[]{:S(2)}) copy-start(s32[8]{0:T(128)S(1)} %get-tuple-element.44.refs_0_) | copy-start | bytes 100
  189.7 4.9 %copy-start.1 = (f32[4,2,256,256]{3,2,1,0:T(8,128)S(1)}, f32[4,2,256,256]{3,2,1,0:T(8,128)}, u32[]{:S(2)}) copy-start(f32[4,2,256,256]{3,2,1,0:T(8,128)} %get-tuple-element.28) | copy-start | bytes 6291460
  194.6 4.0 %copy-start.2 = (f32[2,256,256]{2,1,0:T(8,128)S(1)}, f32[2,256,256]{2,1,0:T(8,128)}, u32[]{:S(2)}) copy-start(f32[2,256,256]{2,1,0:T(8,128)} %shard_map.126) | copy-start | bytes 1572868
  225.2 3.7 %copy-start.4 = (f32[4,2,32,256]{3,2,1,0:T(8,128)S(1)}, f32[4,2,32,256]{3,2,1,0:T(8,128)}, u32[]{:S(2)}) copy-start(f32[4,2,32,256]{3,2,1,0:T(8,128)} %get-tuple-element.31) | copy-start | bytes 786436
  227.2 18.6 %copy-start.3 = (f32[1,256,256]{2,1,0:T(8,128)S(1)}, f32[1,256,256]{2,1,0:T(8,128)}, u32[]{:S(2)}) copy-start(f32[1,256,256]{2,1,0:T(8,128)} %param.16) | copy-start | bytes 786436
  228.8 17.8 %copy-start.7 = (f32[8,32,256]{2,1,0:T(8,128)S(1)}, f32[8,32,256]{2,1,0:T(8,128)}, u32[]{:S(2)}) copy-start(f32[8,32,256]{2,1,0:T(8,128)} %get-tuple-element.33) | copy-start | bytes 786436
  244.6 2.8 %copy-start.5 = (f32[4,4,32,256]{3,2,1,0:T(8,128)S(1)}, f32[4,4,32,256]{3,2,1,0:T(8,128)}, u32[]{:S(2)}) copy-start(f32[4,4,32,256]{3,2,1,0:T(8,128)} %get-tuple-element.34) | copy-start | bytes 1572868
  247.5 12.7 %copy-start.6 = (f32[1,256,256]{2,1,0:T(8,128)S(1)}, f32[1,256,256]{2,1,0:T(8,128)}, u32[]{:S(2)}) copy-start(f32[1,256,256]{2,1,0:T(8,128)} %param.19) | copy-start | bytes 786436
